TPU v7x, 32 devices: a whole 2x2x4 slice. The times are simulated.
32 devices in a mesh: groups: 2 (over y), blk: 4 (over z), feat: 2 (over x), sub: 2 (over core).
Axes of the slice: x: 2, y: 2, z: 4, core: 2. Of those that a mesh axis runs over, the one named last changes fastest.
Arguments:
- frames: bfloat16 [16384, 1024], P(('groups', 'blk', 'sub'), 'feat'), parts along dimension 0, may hold values from -6 to 6
- clip_label: int32 [16384], P(('groups', 'blk', 'sub')), parts along dimension 0, may hold values from 0 to 8191, as said below
Outputs:
- duplicate_score: float32 [16384], P(('groups', 'blk', 'sub')), parts along dimension 0
There are 2 independent parts, one for each index of `groups`. A program takes and returns all parts, laid end to end along the dimension named above; each array names one. Nothing has to cross between parts.
Inputs may be any that keep to these rules, and one draw needn't show every extreme that they name: `clip_label`: clip numbers never fall along the frames; a clip's number is the index of its first frame; every clip holds at most 64 frames, and some clip holds exactly 64; the last frame forms a clip of its own.
All inputs are finite; a program needn't handle non-finite values.
Results may differ from a plain program's by a relative error of at most 0.0003.
Values may be sent and summed in bfloat16 or wider, within the bound.
A program may use at most 64 MiB of HBM per device.

v0:
```python
import functools
import math

import jax
import jax.numpy as jnp
from jax import lax
from jax.experimental import pallas as pl
from jax.experimental.pallas import tpu as pltpu
from jax.sharding import PartitionSpec as P

softness_level = 0.5
masked_value = -1e30
MESH = pl.DeviceIdType.MESH
LANES = 128
ROW_BLOCK = 256


def kernel(
    sizes,
    x_ref,
    label_hbm,
    out_ref,
    queries,
    partner_keys,
    next_keys,
    labels,
    label_ref,
    query_label,
    row_peak,
    row_total,
    col_peak,
    col_total,
    row_parts,
    col_out,
    col_parts,
    local_sem,
    label_sem,
    x_send,
    x_recv,
    z_send,
    z_recv,
    own_send,
    own_recv,
    fwd_send,
    fwd_recv,
    label_send,
    label_recv,
    row_send,
    row_recv,
    col_send,
    col_recv,
):
    cycle, feats, reach, rows, width, chunk = sizes
    piece = rows // feats
    n_key = piece // chunk
    n_all = rows // chunk
    factor = math.log2(math.e) / (math.sqrt(width * feats) * softness_level)
    blk = lax.axis_index("blk")
    feat = lax.axis_index("feat")
    sub = lax.axis_index("sub")
    other = 1 - sub

    def ahead(d):
        return lax.rem(blk + d, cycle)

    def behind(d):
        return lax.rem(blk + cycle - d, cycle)

    def peer(o):
        return lax.rem(feat + o, feats)

    def chunk_rows(owner, k):
        start = lax.rem(owner * piece + k * chunk, rows)
        return pl.ds(pl.multiple_of(start, chunk), chunk)

    def cols(q):
        return pl.ds(pl.multiple_of(q * width, width), width)

    def features(q, r):
        return queries.at[r, cols(q)]

    def send(src, dst, ssem, rsem, **where):
        return pltpu.make_async_remote_copy(
            src_ref=src, dst_ref=dst, send_sem=ssem, recv_sem=rsem,
            device_id=where, device_id_type=MESH,
        )

    key_rows = pl.ds(pl.multiple_of(feat * piece, piece), piece)

    def x_copy(o, k):
        to = peer(o)
        r = chunk_rows(to, k)
        return send(x_ref.at[r], features(feat, r), x_send.at[o, k], x_recv.at[feat, k], feat=to)

    def x_arrival(o, k):
        q = peer(o)
        r = chunk_rows(feat, k)
        return send(x_ref.at[r], features(q, r), x_send.at[o, k], x_recv.at[q, k], feat=q)

    def key_part(q, k, held):
        r = chunk_rows(feat, k)
        return features(q, r) if held else x_ref.at[r]

    def z_copy(d, q, k, held):
        return send(
            key_part(q, k, held), next_keys.at[d - 1, k, sub, :, cols(q)],
            z_send.at[d - 1, q, k], z_recv.at[d - 1, q, k], blk=behind(d),
        )

    def own_copy(q, k, held):
        return send(
            key_part(q, k, held), partner_keys.at[pl.ds(k * chunk, chunk), cols(q)],
            own_send.at[q, k], own_recv.at[q, k], sub=other,
        )

    def fwd_copy(d, q, k, origin):
        part = next_keys.at[d - 1, k, origin, :, cols(q)]
        return send(
            part, part, fwd_send.at[d - 1, q, k], fwd_recv.at[d - 1, q, k], sub=other
        )

    def label_slot(d, origin):
        return 1 + 2 * (d - 1) + origin

    def label_copy(d, turn, slot):
        to = sub if turn == 0 else other
        return send(
            label_hbm, labels.at[slot], label_send.at[label_slot(d, turn)],
            label_recv.at[slot], blk=behind(d), sub=to,
        )

    def partner_label():
        return send(label_hbm, labels.at[0], label_send.at[0], label_recv.at[0], sub=other)

    def row_copy(o, slot):
        return send(
            row_parts.at[slot], row_parts.at[slot], row_send.at[o], row_recv.at[slot],
            feat=peer(o),
        )

    def col_copy(d, f, t, slot_f, slot_s):
        return send(
            col_out.at[d - 1, t], col_parts.at[d - 1, slot_f, slot_s],
            col_send.at[d - 1, f, t], col_recv.at[d - 1, slot_f, slot_s],
            blk=ahead(d), feat=f, sub=t,
        )

    local = pltpu.make_async_copy(x_ref, queries.at[:, cols(feat)], local_sem)
    local.start()
    local_label = pltpu.make_async_copy(label_hbm, label_ref, label_sem)
    local_label.start()

    barrier = pltpu.get_barrier_semaphore()
    pl.semaphore_signal(barrier, inc=1, device_id={"sub": other}, device_id_type=MESH)
    for o in range(1, feats):
        pl.semaphore_signal(barrier, inc=1, device_id={"feat": peer(o)}, device_id_type=MESH)
    for d in range(1, reach + 1):
        for b in (ahead(d), behind(d)):
            for f in range(feats):
                for t in range(2):
                    pl.semaphore_signal(
                        barrier, inc=1, device_id={"blk": b, "feat": f, "sub": t},
                        device_id_type=MESH,
                    )
    pl.semaphore_wait(barrier, feats + 4 * reach * feats)

    sends = []

    def go(copy):
        copy.start()
        sends.append(copy)

    for k in range(n_all):
        for o in range(1, feats):
            go(x_copy(o, k))
        if k < n_key:
            for d in range(1, reach + 1):
                go(z_copy(d, feat, k, False))
            go(own_copy(feat, k, False))
    go(partner_label())
    for d in range(1, reach + 1):
        for turn in range(2):
            go(label_copy(d, turn, label_slot(d, sub)))

    local_label.wait()
    row_peak[...] = jnp.full_like(row_peak, masked_value)
    row_total[...] = jnp.zeros_like(row_total)
    col_peak[...] = jnp.full_like(col_peak, masked_value)
    col_total[...] = jnp.zeros_like(col_total)
    for i in range(rows // LANES):
        line = label_ref[:, i * LANES : (i + 1) * LANES].astype(jnp.float32)
        query_label[i * LANES : (i + 1) * LANES, :] = jnp.broadcast_to(line, (LANES, LANES)).T

    def tile(start, count, keys, lines, column):
        groups = len(lines)
        block = min(ROW_BLOCK, count)
        parts = block // 8
        lane = [slice(b * LANES, (b + 1) * LANES) for b in range(groups)]

        def one(i, carry):
            there = pl.ds(pl.multiple_of(start + i * block, block), block)
            score = lax.dot_general(
                queries[there, :], keys(), (((1,), (1,)), ((), ())),
                preferred_element_type=jnp.float32,
            )
            mine = query_label[there, :]
            values = [
                jnp.where(mine != lines[b], score[:, lane[b]] * factor, masked_value)
                for b in range(groups)
            ]
            old = row_peak[there, :]
            new = functools.reduce(jnp.maximum, values, old)
            row_peak[there, :] = new
            row_total[there, :] = functools.reduce(
                jnp.add,
                [jnp.exp2(v - new) for v in values],
                row_total[there, :] * jnp.exp2(old - new),
            )
            if column is not None:
                d, j = column
                for b in range(groups):
                    v = values[b].reshape(parts, 8, LANES)
                    old_c = col_peak[d - 1, j, :, lane[b]]
                    new_c = jnp.maximum(old_c, jnp.max(v, axis=0))
                    col_peak[d - 1, j, :, lane[b]] = new_c
                    col_total[d - 1, j, :, lane[b]] = col_total[
                        d - 1, j, :, lane[b]
                    ] * jnp.exp2(old_c - new_c) + jnp.sum(jnp.exp2(v - new_c[None]), axis=0)
            return carry

        lax.fori_loop(0, count // block, one, 0, unroll=True)

    for k in range(n_key):
        for o in range(1, feats):
            q = peer(o)
            x_arrival(o, k).wait_recv()
            for d in range(1, reach + 1):
                go(z_copy(d, q, k, True))
            go(own_copy(q, k, True))
    for k in range(n_key):
        for d in range(1, reach + 1):
            z_copy(d, feat, k, False).wait_recv()
            go(fwd_copy(d, feat, k, sub))

    local.wait()
    partner_label().wait_recv()
    for d in range(1, reach + 1):
        label_copy(d, 0, label_slot(d, sub)).wait_recv()
        label_copy(d, 1, label_slot(d, other)).wait_recv()

    def key_lines(line):
        return [line[:, b * LANES : (b + 1) * LANES] for b in range(line.shape[1] // LANES)]

    own_lines = key_lines(label_ref[:, key_rows].astype(jnp.float32))
    beside_lines = key_lines(labels[0, :, key_rows].astype(jnp.float32))
    first_row = pl.multiple_of(feat * piece, piece)

    def own_tile(start, count):
        tile(start, count, lambda: queries[key_rows, :], own_lines, None)

    def beside_tile(start, count):
        tile(start, count, lambda: partner_keys[...], beside_lines, None)

    def next_tile(start, count, d, j):
        r = pl.ds(pl.multiple_of(feat * piece + j * chunk, chunk), chunk)
        lines = []
        for t in range(2):
            lines += key_lines(labels[label_slot(d, t), :, r].astype(jnp.float32))
        keys = lambda: next_keys[d - 1, j].reshape(2 * chunk, width * feats)
        tile(start, count, keys, lines, (d, j))

    def rotated(k):
        return pl.multiple_of(lax.rem(feat * piece + k * chunk, rows), chunk)

    own_tile(first_row, piece)
    for k in range(n_key):
        for q in range(feats):
            own_copy(q, k, False).wait_recv()
    beside_tile(first_row, piece)

    def relay(j):
        for d in range(1, reach + 1):
            for o in range(1, feats):
                z_copy(d, peer(o), j, False).wait_recv()
                go(fwd_copy(d, peer(o), j, sub))

    def key_chunk(j, upto):
        for d in range(1, reach + 1):
            for q in range(feats):
                fwd_copy(d, q, j, other).wait_recv()
            tall = max(h for h in range(1, n_key + 1) if upto % h == 0 and n_key % h == 0)

            def step(i, carry):
                next_tile(rotated(i * tall), tall * chunk, d, j)
                return carry

            lax.fori_loop(0, upto // tall, step, 0, unroll=True)

    relayed, scored, owned = 0, 0, n_key
    for k in range(n_key, n_all):
        if scored < relayed:
            key_chunk(scored, k)
            scored += 1
        for o in range(1, feats):
            x_arrival(o, k).wait_recv()
        if relayed < n_key:
            relay(relayed)
            relayed += 1
        start = rotated(k)
        for d in range(1, reach + 1):
            for j in range(scored):
                next_tile(start, chunk, d, j)
        if n_key % 2 == 0 and k + 1 - owned == 2 and k + 1 < n_all:
            own_tile(rotated(owned), 2 * chunk)
            beside_tile(rotated(owned), 2 * chunk)
            owned += 2
    while relayed < n_key:
        relay(relayed)
        relayed += 1
    left = 2 if n_key % 2 == 0 else 1
    for k in range(owned, n_all, left):
        own_tile(rotated(k), left * chunk)
        beside_tile(rotated(k), left * chunk)
    while scored < n_key:
        key_chunk(scored, n_all)
        scored += 1

    for d in range(1, reach + 1):
        for t in range(2):
            for j in range(n_key):
                part = slice(t * chunk, (t + 1) * chunk)
                peaks = col_peak[d - 1, j, :, part]
                top = jnp.max(peaks, axis=0, keepdims=True)
                total = jnp.sum(
                    col_total[d - 1, j, :, part] * jnp.exp2(peaks - top), axis=0, keepdims=True
                )
                col_out[d - 1, t, :, j * chunk : (j + 1) * chunk] = (
                    top * math.log(2.0) + jnp.log(total)
                )
            for f in range(feats):
                go(col_copy(d, f, t, feat, sub))
    for i in range(rows // LANES):
        here = slice(i * LANES, (i + 1) * LANES)
        peaks = row_peak[here, :].T
        top = jnp.max(peaks, axis=0, keepdims=True)
        total = jnp.sum(row_total[here, :].T * jnp.exp2(peaks - top), axis=0, keepdims=True)
        row_parts[feat, :, here] = top * math.log(2.0) + jnp.log(total)
    for o in range(1, feats):
        go(row_copy(o, feat))

    for o in range(1, feats):
        row_copy(o, peer(o)).wait_recv()
    for d in range(1, reach + 1):
        for f in range(feats):
            for t in range(2):
                col_copy(d, f, t, f, t).wait_recv()

    shift = math.log((2 * reach + 1) * rows * 2)
    for f in range(feats):
        here = slice(f * piece, (f + 1) * piece)
        parts = [row_parts[q, :, here] for q in range(feats)]
        parts += [col_parts[d, f, t] for d in range(reach) for t in range(2)]
        top = functools.reduce(jnp.maximum, parts)
        total = functools.reduce(jnp.add, [jnp.exp(v - top) for v in parts])
        out_ref[:, here] = softness_level * (top + jnp.log(total) - shift)

    for copy in sends:
        copy.wait_send()


def solution(mesh):
    cycle, feats = mesh.shape["blk"], mesh.shape["feat"]
    reach = min(4, (cycle - 1) // 2)

    def body(frames, clip_label):
        rows, width = frames.shape
        piece = rows // feats
        chunk = min(128, piece)
        n_key, n_all = piece // chunk, rows // chunk
        dma = pltpu.SemaphoreType.DMA
        sizes = (cycle, feats, reach, rows, width, chunk)
        out = pl.pallas_call(
            functools.partial(kernel, sizes),
            out_shape=jax.ShapeDtypeStruct((1, rows), jnp.float32),
            in_specs=[
                pl.BlockSpec(memory_space=pltpu.HBM),
                pl.BlockSpec(memory_space=pltpu.HBM),
            ],
            out_specs=pl.BlockSpec(memory_space=pltpu.VMEM),
            scratch_shapes=[
                pltpu.VMEM((rows, feats * width), frames.dtype),
                pltpu.VMEM((piece, feats * width), frames.dtype),
                pltpu.VMEM((reach, n_key, 2, chunk, feats * width), frames.dtype),
                pltpu.VMEM((1 + 2 * reach, 1, rows), jnp.int32),
                pltpu.VMEM((1, rows), jnp.int32),
                pltpu.VMEM((rows, LANES), jnp.float32),
                pltpu.VMEM((rows, LANES), jnp.float32),
                pltpu.VMEM((rows, LANES), jnp.float32),
                pltpu.VMEM((reach, n_key, 8, 2 * chunk), jnp.float32),
                pltpu.VMEM((reach, n_key, 8, 2 * chunk), jnp.float32),
                pltpu.VMEM((feats, 1, rows), jnp.float32),
                pltpu.VMEM((reach, 2, 1, piece), jnp.float32),
                pltpu.VMEM((reach, feats, 2, 1, piece), jnp.float32),
                dma,
                dma,
                dma((feats, n_all)),
                dma((feats, n_all)),
                dma((reach, feats, n_key)),
                dma((reach, feats, n_key)),
                dma((feats, n_key)),
                dma((feats, n_key)),
                dma((reach, feats, n_key)),
                dma((reach, feats, n_key)),
                dma((1 + 2 * reach,)),
                dma((1 + 2 * reach,)),
                dma((feats,)),
                dma((feats,)),
                dma((reach, feats, 2)),
                dma((reach, feats, 2)),
            ],
            compiler_params=pltpu.CompilerParams(
                collective_id=0, has_side_effects=True, vmem_limit_bytes=63 * 1024 * 1024
            ),
            name="chamfer",
        )(frames, clip_label.reshape(1, rows))
        return out.reshape(rows)

    in_specs = (P(("groups", "blk", "sub"), "feat"), P(("groups", "blk", "sub")))
    out_specs = P(("groups", "blk", "sub"))
    return jax.shard_map(body, mesh=mesh, in_specs=in_specs, out_specs=out_specs, check_vma=False)
```

profile of v0, /device:TPU:0, one launch (start us, length us, event | category | flops | bytes accessed | tf_op | source)
XLA Modules:
  0.0 40.7 jit_solution(10383300951419516272)
XLA Ops:
  0.0 39.5 %chamfer.1 = f32[1,1024]{1,0:T(1,128)} custom-call(bf16[1024,512]{1,0:T(8,128)(2,1)} %x_ref.1, s32[1,1024]{1,0:T(1,128)} %bitcast.3), custom_call_target="tpu_custom_call" | custom-call | tf_op jit(solution)/shard_map/chamfer/pallas_call | solution.py:382
  39.5 1.3 %copy.4 = f32[1024]{0:T(1024)} copy(f32[1024]{0:T(1024)} %bitcast.2) | data formatting | bytes 8192
where the time goes:
time: 40.9 us; the launch traced here: 40.7 us
  Pallas kernels  39.5 us (97%)
  local copies, waits for them, and re-layouts  1.28 us (3%)
    pallas_call x1, Pallas kernels, body(): pl.pallas_call(functools.partial(kernel, sizes), out_shape=jax.ShapeDtype...  39.5 us
    unnamed x1, local copies, waits for them, and re-layouts  1.28 us

commit v1 on v0

--- a/solution.py
+++ b/solution.py
@@ -104,7 +104,7 @@
     def z_copy(d, q, k, held):
         return send(
             key_part(q, k, held), next_keys.at[d - 1, k, sub, :, cols(q)],
-            z_send.at[d - 1, q, k], z_recv.at[d - 1, q, k], blk=behind(d),
+            z_send.at[d - 1, q, k], z_recv.at[d - 1, q, k], blk=ahead(d),
         )
 
     def own_copy(q, k, held):
@@ -126,7 +126,7 @@
         to = sub if turn == 0 else other
         return send(
             label_hbm, labels.at[slot], label_send.at[label_slot(d, turn)],
-            label_recv.at[slot], blk=behind(d), sub=to,
+            label_recv.at[slot], blk=ahead(d), sub=to,
         )
 
     def partner_label():
@@ -142,7 +142,7 @@
         return send(
             col_out.at[d - 1, t], col_parts.at[d - 1, slot_f, slot_s],
             col_send.at[d - 1, f, t], col_recv.at[d - 1, slot_f, slot_s],
-            blk=ahead(d), feat=f, sub=t,
+            blk=behind(d), feat=f, sub=t,
         )
 
     local = pltpu.make_async_copy(x_ref, queries.at[:, cols(feat)], local_sem)
@@ -155,14 +155,11 @@
     for o in range(1, feats):
         pl.semaphore_signal(barrier, inc=1, device_id={"feat": peer(o)}, device_id_type=MESH)
     for d in range(1, reach + 1):
-        for b in (ahead(d), behind(d)):
-            for f in range(feats):
-                for t in range(2):
-                    pl.semaphore_signal(
-                        barrier, inc=1, device_id={"blk": b, "feat": f, "sub": t},
-                        device_id_type=MESH,
-                    )
-    pl.semaphore_wait(barrier, feats + 4 * reach * feats)
+        for t in range(2):
+            pl.semaphore_signal(
+                barrier, inc=1, device_id={"blk": behind(d), "sub": t}, device_id_type=MESH
+            )
+    pl.semaphore_wait(barrier, feats + 2 * reach)
 
     sends = []
 

time: 40.9 us -> 38.5 us (0.941)
  Pallas kernels: 39.5 us -> 37.1 us
    pallas_call x1, Pallas kernels: 39.5 us -> 37.1 us  [body(): pl.pallas_call(functools.partial(kernel, sizes), out_shape=jax.ShapeDtype...]
where the time goes in v1:
time: 38.5 us; the launch traced here: 38.4 us
  Pallas kernels  37.1 us (96%)
  local copies, waits for them, and re-layouts  1.28 us (3%)
    pallas_call x1, Pallas kernels, body(): pl.pallas_call(functools.partial(kernel, sizes), out_shape=jax.ShapeDtype...  37.1 us
    unnamed x1, local copies, waits for them, and re-layouts  1.28 us

profile of v1, /device:TPU:0, one launch (start us, length us, event | category | flops | bytes accessed | tf_op | source)
XLA Modules:
  0.0 38.4 jit_solution(16550405882079473699)
XLA Ops:
  0.0 37.1 %chamfer.1 = f32[1,1024]{1,0:T(1,128)} custom-call(bf16[1024,512]{1,0:T(8,128)(2,1)} %x_ref.1, s32[1,1024]{1,0:T(1,128)} %bitcast.3), custom_call_target="tpu_custom_call" | custom-call | tf_op jit(solution)/shard_map/chamfer/pallas_call | solution.py:379
  37.1 1.3 %copy.4 = f32[1024]{0:T(1024)} copy(f32[1024]{0:T(1024)} %bitcast.2) | data formatting | bytes 8192

commit v2 on v1

v2 whole, which is shorter than its diff:
```python
import functools
import math

import jax
import jax.numpy as jnp
from jax import lax
from jax.experimental import pallas as pl
from jax.experimental.pallas import tpu as pltpu
from jax.sharding import PartitionSpec as P

softness_level = 0.5
masked_value = -1e30
MESH = pl.DeviceIdType.MESH
LANES = 128
KEY_BLOCK = 256


def kernel(
    sizes,
    x_ref,
    label_hbm,
    out_ref,
    queries,
    next_keys,
    labels,
    query_line,
    own_label,
    next_label,
    row_peak,
    row_total,
    col_peak,
    col_total,
    row_out,
    row_parts,
    col_out,
    col_parts,
    local_sem,
    x_send,
    x_recv,
    z_send,
    z_recv,
    sub_send,
    sub_recv,
    label_send,
    label_recv,
    row_send,
    row_recv,
    col_send,
    col_recv,
):
    cycle, feats, reach, rows, width, chunk = sizes
    piece = rows // feats
    n_key = piece // chunk
    n_all = rows // chunk
    group = 2 if n_key % 2 == 0 else 1
    factor = math.log2(math.e) / (math.sqrt(width * feats) * softness_level)
    blk = lax.axis_index("blk")
    feat = lax.axis_index("feat")
    sub = lax.axis_index("sub")
    other = 1 - sub

    def ahead(d):
        return lax.rem(blk + d, cycle)

    def behind(d):
        return lax.rem(blk + cycle - d, cycle)

    def peer(o):
        return lax.rem(feat + o, feats)

    def chunk_rows(owner, k, count=1):
        start = lax.rem(owner * piece + k * chunk, rows)
        return pl.ds(pl.multiple_of(start, chunk * count), chunk * count)

    def cols(q):
        return pl.ds(pl.multiple_of(q * width, width), width)

    def send(src, dst, ssem, rsem, **where):
        return pltpu.make_async_remote_copy(
            src_ref=src, dst_ref=dst, send_sem=ssem, recv_sem=rsem,
            device_id=where, device_id_type=MESH,
        )

    def x_copy(o, k):
        to = peer(o)
        r = chunk_rows(to, k)
        return send(
            x_ref.at[r], queries.at[0, r, cols(feat)], x_send.at[o, k], x_recv.at[feat, k],
            feat=to,
        )

    def x_arrival(o, k):
        q = peer(o)
        r = chunk_rows(feat, k)
        return send(
            x_ref.at[r], queries.at[0, r, cols(q)], x_send.at[o, k], x_recv.at[q, k], feat=q
        )

    def part(q, k, held):
        r = chunk_rows(feat, k)
        return queries.at[0, r, cols(q)] if held else x_ref.at[r]

    def z_copy(d, q, k, held):
        return send(
            part(q, k, held), next_keys.at[d - 1, k, :, cols(q)],
            z_send.at[d - 1, q, k], z_recv.at[d - 1, q, k], blk=ahead(d),
        )

    def sub_copy(q, k, held):
        return send(
            part(q, k, held), queries.at[1, chunk_rows(feat, k), cols(q)],
            sub_send.at[q, k], sub_recv.at[q, k], sub=other,
        )

    def label_copy(slot):
        where = {"sub": other} if slot == 1 else {"blk": ahead(slot - 1)}
        return send(label_hbm, labels.at[slot], label_send.at[slot], label_recv.at[slot], **where)

    def row_copy(o, half, slot_f, slot_s):
        src = row_out if half else row_parts.at[slot_f, slot_s]
        return send(
            src, row_parts.at[slot_f, slot_s], row_send.at[o, half], row_recv.at[slot_f, slot_s],
            feat=peer(o), sub=other if half else sub,
        )

    def col_copy(d, f, slot_f):
        return send(
            col_out.at[d - 1], col_parts.at[d - 1, slot_f], col_send.at[d - 1, f],
            col_recv.at[d - 1, slot_f], blk=behind(d), feat=f,
        )

    local = pltpu.make_async_copy(x_ref, queries.at[0, :, cols(feat)], local_sem.at[0])
    local.start()
    local_label = pltpu.make_async_copy(label_hbm, labels.at[0], local_sem.at[1])
    local_label.start()

    barrier = pltpu.get_barrier_semaphore()
    pl.semaphore_signal(barrier, inc=1, device_id={"sub": other}, device_id_type=MESH)
    for o in range(1, feats):
        pl.semaphore_signal(barrier, inc=1, device_id={"feat": peer(o)}, device_id_type=MESH)
    for d in range(1, reach + 1):
        pl.semaphore_signal(barrier, inc=1, device_id={"blk": behind(d)}, device_id_type=MESH)
    pl.semaphore_wait(barrier, feats + reach)

    sends = []

    def go(copy):
        copy.start()
        sends.append(copy)

    for k in range(n_all):
        for o in range(1, feats):
            go(x_copy(o, k))
        if k < n_key:
            for d in range(1, reach + 1):
                go(z_copy(d, feat, k, False))
    for slot in range(1, 2 + reach):
        go(label_copy(slot))
    for k in range(n_all):
        go(sub_copy(feat, k, False))

    row_peak[...] = jnp.full_like(row_peak, masked_value)
    row_total[...] = jnp.zeros_like(row_total)
    col_peak[...] = jnp.full_like(col_peak, masked_value)
    col_total[...] = jnp.zeros_like(col_total)

    def down(slot, k):
        line = labels[slot, :, chunk_rows(feat, k)].astype(jnp.float32)
        return jnp.broadcast_to(line, (LANES, chunk)).T

    def across(slot, s):
        for k in range(n_all):
            line = labels[slot, :, chunk_rows(feat, k)].astype(jnp.float32)
            query_line[s, k] = jnp.broadcast_to(line, (8, chunk))

    def tile(s, u, keys, key_label, column):
        count = keys.shape[0]
        block = min(KEY_BLOCK, count)
        q = queries[s, chunk_rows(feat, u * group, group), :]
        lane = [slice(b * chunk, (b + 1) * chunk) for b in range(group)]
        for m in range(0, count, block):
            here = slice(m, m + block)
            score = lax.dot_general(
                keys[here, :], q, (((1,), (1,)), ((), ())), preferred_element_type=jnp.float32
            )
            mine = key_label[here, :]
            values = []
            for b in range(group):
                k = u * group + b
                line = query_line[s, k]
                apart = mine.reshape(block // 8, 8, chunk) != line[None]
                v = jnp.where(
                    apart, (score[:, lane[b]] * factor).reshape(block // 8, 8, chunk), masked_value
                )
                values.append(v)
                old = row_peak[s, k]
                new = jnp.maximum(old, jnp.max(v, axis=0))
                row_peak[s, k] = new
                row_total[s, k] = row_total[s, k] * jnp.exp2(old - new) + jnp.sum(
                    jnp.exp2(v - new[None]), axis=0
                )
            if column is not None:
                peak, total = column
                values = [v.reshape(block, chunk) for v in values]
                old = peak[here, :]
                new = functools.reduce(jnp.maximum, values, old)
                peak[here, :] = new
                total[here, :] = functools.reduce(
                    jnp.add,
                    [jnp.exp2(v - new) for v in values],
                    total[here, :] * jnp.exp2(old - new),
                )

    def own_tile(s, u):
        tile(s, u, queries.at[0, chunk_rows(feat, 0, n_key)], own_label, None)

    def next_tile(s, u, d, j):
        here = pl.ds(j * chunk, chunk)
        tile(
            s, u, next_keys.at[d - 1, j], next_label.at[d - 1, here],
            (col_peak.at[d - 1, here], col_total.at[d - 1, here]),
        )

    done, taken = [], []

    def take_x(k):
        for o in range(1, feats):
            q = peer(o)
            x_arrival(o, k).wait_recv()
            if k < n_key:
                for d in range(1, reach + 1):
                    go(z_copy(d, q, k, True))
            go(sub_copy(q, k, True))

    def take_sub(k):
        for o in range(feats):
            sub_copy(peer(o), k, False).wait_recv()

    def take_queries(s, units):
        for u in units:
            own_tile(s, u)
            for d, j in taken:
                next_tile(s, u, d, j)
            done.append((s, u))

    def take_keys(j):
        for d in range(1, reach + 1):
            for q in range(feats):
                z_copy(d, q, j, False).wait_recv()
            for s, u in done:
                next_tile(s, u, d, j)
            taken.append((d, j))

    def finish_columns(j):
        for d in range(1, reach + 1):
            here = pl.ds(j * chunk, chunk)
            peaks = col_peak[d - 1, here, :].T
            top = jnp.max(peaks, axis=0, keepdims=True)
            total = jnp.sum(
                col_total[d - 1, here, :].T * jnp.exp2(peaks - top), axis=0, keepdims=True
            )
            col_out[d - 1, :, here] = top * math.log(2.0) + jnp.log(total)

    def finish_rows(s):
        for k in range(n_all):
            peaks = row_peak[s, k]
            top = jnp.max(peaks, axis=0, keepdims=True)
            total = jnp.sum(row_total[s, k] * jnp.exp2(peaks - top), axis=0, keepdims=True)
            value = top * math.log(2.0) + jnp.log(total)
            if s:
                row_out[:, chunk_rows(feat, k)] = value
            else:
                row_parts[feat, sub, :, chunk_rows(feat, k)] = value

    local_label.wait()
    across(0, 0)
    for k in range(n_key):
        own_label[k * chunk : (k + 1) * chunk, :] = down(0, k)
    label_copy(1).wait_recv()
    across(1, 1)
    for d in range(1, reach + 1):
        label_copy(1 + d).wait_recv()
        for k in range(n_key):
            next_label[d - 1, k * chunk : (k + 1) * chunk, :] = down(1 + d, k)

    for k in range(n_key):
        take_x(k)
    local.wait()
    first = range(n_key // group)
    take_queries(0, first)
    for k in range(n_key):
        take_sub(k)
    take_queries(1, first)

    steps = (n_all - n_key) // group
    ready = 0

    def catch_up(upto):
        nonlocal ready
        while ready < upto:
            take_keys(ready)
            ready += 1

    for i in range(steps):
        u = n_key // group + i
        for b in range(group):
            if b == group - 1 and i == steps - 1:
                catch_up(n_key - 1)
            take_x(u * group + b)
        take_queries(0, [u])
        for b in range(group):
            take_sub(u * group + b)
        take_queries(1, [u])
        catch_up(n_key * (i + 1) // steps if i < steps - 1 else n_key - 1)
    for j in range(n_key - 1):
        finish_columns(j)
    catch_up(n_key)

    finish_rows(1)
    for o in range(feats):
        go(row_copy(o, 1, feat, sub))
    finish_rows(0)
    for o in range(1, feats):
        go(row_copy(o, 0, feat, sub))
    finish_columns(n_key - 1)
    for d in range(1, reach + 1):
        for f in range(feats):
            go(col_copy(d, f, feat))

    for o in range(feats):
        for s in range(2):
            if o or s:
                row_copy(o, s, peer(o), other if s else sub).wait_recv()
    for d in range(1, reach + 1):
        for f in range(feats):
            col_copy(d, f, f).wait_recv()

    shift = math.log((2 * reach + 1) * rows * 2)
    for f in range(feats):
        here = slice(f * piece, (f + 1) * piece)
        parts = [row_parts[q, s, :, here] for q in range(feats) for s in range(2)]
        parts += [col_parts[d, f] for d in range(reach)]
        top = functools.reduce(jnp.maximum, parts)
        total = functools.reduce(jnp.add, [jnp.exp(v - top) for v in parts])
        out_ref[:, here] = softness_level * (top + jnp.log(total) - shift)

    for copy in sends:
        copy.wait_send()


def solution(mesh):
    cycle, feats = mesh.shape["blk"], mesh.shape["feat"]
    reach = min(4, (cycle - 1) // 2)

    def body(frames, clip_label):
        rows, width = frames.shape
        piece = rows // feats
        chunk = min(LANES, piece)
        n_key, n_all = piece // chunk, rows // chunk
        dma = pltpu.SemaphoreType.DMA
        f32 = jnp.float32
        sizes = (cycle, feats, reach, rows, width, chunk)
        out = pl.pallas_call(
            functools.partial(kernel, sizes),
            out_shape=jax.ShapeDtypeStruct((1, rows), f32),
            in_specs=[
                pl.BlockSpec(memory_space=pltpu.HBM),
                pl.BlockSpec(memory_space=pltpu.HBM),
            ],
            out_specs=pl.BlockSpec(memory_space=pltpu.VMEM),
            scratch_shapes=[
                pltpu.VMEM((2, rows, feats * width), frames.dtype),
                pltpu.VMEM((reach, n_key, chunk, feats * width), frames.dtype),
                pltpu.VMEM((2 + reach, 1, rows), jnp.int32),
                pltpu.VMEM((2, n_all, 8, chunk), f32),
                pltpu.VMEM((piece, LANES), f32),
                pltpu.VMEM((reach, piece, LANES), f32),
                pltpu.VMEM((2, n_all, 8, chunk), f32),
                pltpu.VMEM((2, n_all, 8, chunk), f32),
                pltpu.VMEM((reach, piece, LANES), f32),
                pltpu.VMEM((reach, piece, LANES), f32),
                pltpu.VMEM((1, rows), f32),
                pltpu.VMEM((feats, 2, 1, rows), f32),
                pltpu.VMEM((reach, 1, piece), f32),
                pltpu.VMEM((reach, feats, 1, piece), f32),
                dma((2,)),
                dma((feats, n_all)),
                dma((feats, n_all)),
                dma((reach, feats, n_key)),
                dma((reach, feats, n_key)),
                dma((feats, n_all)),
                dma((feats, n_all)),
                dma((2 + reach,)),
                dma((2 + reach,)),
                dma((feats, 2)),
                dma((feats, 2)),
                dma((reach, feats)),
                dma((reach, feats)),
            ],
            compiler_params=pltpu.CompilerParams(
                collective_id=0, has_side_effects=True, vmem_limit_bytes=63 * 1024 * 1024
            ),
            name="chamfer",
        )(frames, clip_label.reshape(1, rows))
        return out.reshape(rows)

    in_specs = (P(("groups", "blk", "sub"), "feat"), P(("groups", "blk", "sub")))
    out_specs = P(("groups", "blk", "sub"))
    return jax.shard_map(body, mesh=mesh, in_specs=in_specs, out_specs=out_specs, check_vma=False)
```

time: 38.5 us -> 41.3 us (1.073)
  Pallas kernels: 37.1 us -> 39.8 us
    pallas_call x1, Pallas kernels: 37.1 us -> 39.8 us  [body(): pl.pallas_call(functools.partial(kernel, sizes), out_shape=jax.ShapeDtype...]
where the time goes in v2:
time: 41.3 us; the launch traced here: 41.1 us
  Pallas kernels  39.8 us (96%)
  local copies, waits for them, and re-layouts  1.28 us (3%)
    pallas_call x1, Pallas kernels, body(): pl.pallas_call(functools.partial(kernel, sizes), out_shape=jax.ShapeDtype...  39.8 us
    unnamed x1, local copies, waits for them, and re-layouts  1.28 us

profile of v2, /device:TPU:0, one launch (start us, length us, event | category | flops | bytes accessed | tf_op | source)
XLA Modules:
  0.0 41.1 jit_solution(9337494563301835966)
XLA Ops:
  0.0 39.8 %chamfer.1 = f32[1,1024]{1,0:T(1,128)} custom-call(bf16[1024,512]{1,0:T(8,128)(2,1)} %x_ref.1, s32[1,1024]{1,0:T(1,128)} %bitcast.3), custom_call_target="tpu_custom_call" | custom-call | tf_op jit(solution)/shard_map/chamfer/pallas_call | solution.py:363
  39.8 1.3 %copy.4 = f32[1024]{0:T(1024)} copy(f32[1024]{0:T(1024)} %bitcast.2) | data formatting | bytes 8192

commit v3 on v2

--- a/solution.py
+++ b/solution.py
@@ -52,7 +52,6 @@
     piece = rows // feats
     n_key = piece // chunk
     n_all = rows // chunk
-    group = 2 if n_key % 2 == 0 else 1
     factor = math.log2(math.e) / (math.sqrt(width * feats) * softness_level)
     blk = lax.axis_index("blk")
     feat = lax.axis_index("feat")
@@ -102,7 +101,7 @@
 
     def z_copy(d, q, k, held):
         return send(
-            part(q, k, held), next_keys.at[d - 1, k, :, cols(q)],
+            part(q, k, held), next_keys.at[d - 1, pl.ds(k * chunk, chunk), cols(q)],
             z_send.at[d - 1, q, k], z_recv.at[d - 1, q, k], blk=ahead(d),
         )
 
@@ -148,14 +147,14 @@
         copy.start()
         sends.append(copy)
 
+    for slot in range(1, 2 + reach):
+        go(label_copy(slot))
     for k in range(n_all):
         for o in range(1, feats):
             go(x_copy(o, k))
         if k < n_key:
             for d in range(1, reach + 1):
                 go(z_copy(d, feat, k, False))
-    for slot in range(1, 2 + reach):
-        go(label_copy(slot))
     for k in range(n_all):
         go(sub_copy(feat, k, False))
 
@@ -173,24 +172,22 @@
             line = labels[slot, :, chunk_rows(feat, k)].astype(jnp.float32)
             query_line[s, k] = jnp.broadcast_to(line, (8, chunk))
 
-    def tile(s, u, keys, key_label, column):
+    def tile(k, keys, key_label, column):
         count = keys.shape[0]
-        block = min(KEY_BLOCK, count)
-        q = queries[s, chunk_rows(feat, u * group, group), :]
-        lane = [slice(b * chunk, (b + 1) * chunk) for b in range(group)]
-        for m in range(0, count, block):
+        q = queries[:, chunk_rows(feat, k), :].reshape(2 * chunk, width * feats)
+        lane = [slice(s * chunk, (s + 1) * chunk) for s in range(2)]
+        for m in range(0, count, KEY_BLOCK):
+            block = min(KEY_BLOCK, count - m)
             here = slice(m, m + block)
             score = lax.dot_general(
-                keys[here, :], q, (((1,), (1,)), ((), ())), preferred_element_type=jnp.float32
-            )
+                q, keys[here, :], (((1,), (1,)), ((), ())), preferred_element_type=jnp.float32
+            ).T
             mine = key_label[here, :]
             values = []
-            for b in range(group):
-                k = u * group + b
-                line = query_line[s, k]
-                apart = mine.reshape(block // 8, 8, chunk) != line[None]
+            for s in range(2):
+                apart = mine.reshape(block // 8, 8, chunk) != query_line[s, k][None]
                 v = jnp.where(
-                    apart, (score[:, lane[b]] * factor).reshape(block // 8, 8, chunk), masked_value
+                    apart, (score[:, lane[s]] * factor).reshape(block // 8, 8, chunk), masked_value
                 )
                 values.append(v)
                 old = row_peak[s, k]
@@ -211,17 +208,16 @@
                     total[here, :] * jnp.exp2(old - new),
                 )
 
-    def own_tile(s, u):
-        tile(s, u, queries.at[0, chunk_rows(feat, 0, n_key)], own_label, None)
-
-    def next_tile(s, u, d, j):
-        here = pl.ds(j * chunk, chunk)
-        tile(
-            s, u, next_keys.at[d - 1, j], next_label.at[d - 1, here],
-            (col_peak.at[d - 1, here], col_total.at[d - 1, here]),
-        )
-
-    done, taken = [], []
+    def own_tile(k):
+        tile(k, queries.at[0, chunk_rows(feat, 0, n_key)], own_label, None)
+
+    def next_tile(k, j, count):
+        here = pl.ds(j * chunk, count * chunk)
+        for d in range(1, reach + 1):
+            tile(
+                k, next_keys.at[d - 1, here], next_label.at[d - 1, here],
+                (col_peak.at[d - 1, here], col_total.at[d - 1, here]),
+            )
 
     def take_x(k):
         for o in range(1, feats):
@@ -232,24 +228,19 @@
                     go(z_copy(d, q, k, True))
             go(sub_copy(q, k, True))
 
-    def take_sub(k):
+    def take_queries(k, ready):
         for o in range(feats):
             sub_copy(peer(o), k, False).wait_recv()
-
-    def take_queries(s, units):
-        for u in units:
-            own_tile(s, u)
-            for d, j in taken:
-                next_tile(s, u, d, j)
-            done.append((s, u))
-
-    def take_keys(j):
+        own_tile(k)
+        if ready:
+            next_tile(k, 0, ready)
+
+    def take_keys(j, upto):
         for d in range(1, reach + 1):
             for q in range(feats):
                 z_copy(d, q, j, False).wait_recv()
-            for s, u in done:
-                next_tile(s, u, d, j)
-            taken.append((d, j))
+        for k in range(upto):
+            next_tile(k, j, 1)
 
     def finish_columns(j):
         for d in range(1, reach + 1):
@@ -276,45 +267,35 @@
     across(0, 0)
     for k in range(n_key):
         own_label[k * chunk : (k + 1) * chunk, :] = down(0, k)
-    label_copy(1).wait_recv()
-    across(1, 1)
-    for d in range(1, reach + 1):
-        label_copy(1 + d).wait_recv()
-        for k in range(n_key):
-            next_label[d - 1, k * chunk : (k + 1) * chunk, :] = down(1 + d, k)
 
     for k in range(n_key):
         take_x(k)
+        if k == 0:
+            label_copy(1).wait_recv()
+            across(1, 1)
+            for d in range(1, reach + 1):
+                label_copy(1 + d).wait_recv()
+                for k in range(n_key):
+                    next_label[d - 1, k * chunk : (k + 1) * chunk, :] = down(1 + d, k)
     local.wait()
-    first = range(n_key // group)
-    take_queries(0, first)
     for k in range(n_key):
-        take_sub(k)
-    take_queries(1, first)
-
-    steps = (n_all - n_key) // group
-    ready = 0
-
-    def catch_up(upto):
-        nonlocal ready
+        take_queries(k, 0)
+
+    ready, last_key, last = 0, n_key - 1, n_all - 1
+    for k in range(n_key, last):
+        take_x(k)
+        upto = last_key * (k + 1 - n_key) // (last - n_key)
         while ready < upto:
-            take_keys(ready)
+            take_keys(ready, k)
             ready += 1
-
-    for i in range(steps):
-        u = n_key // group + i
-        for b in range(group):
-            if b == group - 1 and i == steps - 1:
-                catch_up(n_key - 1)
-            take_x(u * group + b)
-        take_queries(0, [u])
-        for b in range(group):
-            take_sub(u * group + b)
-        take_queries(1, [u])
-        catch_up(n_key * (i + 1) // steps if i < steps - 1 else n_key - 1)
-    for j in range(n_key - 1):
-        finish_columns(j)
-    catch_up(n_key)
+        take_queries(k, ready)
+    while ready < last_key:
+        take_keys(ready, last)
+        ready += 1
+
+    take_x(last)
+    take_keys(last_key, last)
+    take_queries(last, n_key)
 
     finish_rows(1)
     for o in range(feats):
@@ -322,7 +303,8 @@
     finish_rows(0)
     for o in range(1, feats):
         go(row_copy(o, 0, feat, sub))
-    finish_columns(n_key - 1)
+    for j in range(n_key):
+        finish_columns(j)
     for d in range(1, reach + 1):
         for f in range(feats):
             go(col_copy(d, f, feat))
@@ -370,7 +352,7 @@
             out_specs=pl.BlockSpec(memory_space=pltpu.VMEM),
             scratch_shapes=[
                 pltpu.VMEM((2, rows, feats * width), frames.dtype),
-                pltpu.VMEM((reach, n_key, chunk, feats * width), frames.dtype),
+                pltpu.VMEM((reach, piece, feats * width), frames.dtype),
                 pltpu.VMEM((2 + reach, 1, rows), jnp.int32),
                 pltpu.VMEM((2, n_all, 8, chunk), f32),
                 pltpu.VMEM((piece, LANES), f32),

time: 41.3 us -> 37.7 us (0.913)
  Pallas kernels: 39.8 us -> 36.3 us
    pallas_call x1, Pallas kernels: 39.8 us -> 36.3 us  [body(): pl.pallas_call(functools.partial(kernel, sizes), out_shape=jax.ShapeDtype...]
where the time goes in v3:
time: 37.7 us; the launch traced here: 37.5 us
  Pallas kernels  36.3 us (96%)
  local copies, waits for them, and re-layouts  1.28 us (3%)
    pallas_call x1, Pallas kernels, body(): pl.pallas_call(functools.partial(kernel, sizes), out_shape=jax.ShapeDtype...  36.3 us
    unnamed x1, local copies, waits for them, and re-layouts  1.28 us

profile of v3, /device:TPU:0, one launch (start us, length us, event | category | flops | bytes accessed | tf_op | source)
XLA Modules:
  0.0 37.5 jit_solution(4115707240379577453)
XLA Ops:
  0.0 36.3 %chamfer.1 = f32[1,1024]{1,0:T(1,128)} custom-call(bf16[1024,512]{1,0:T(8,128)(2,1)} %x_ref.1, s32[1,1024]{1,0:T(1,128)} %bitcast.3), custom_call_target="tpu_custom_call" | custom-call | tf_op jit(solution)/shard_map/chamfer/pallas_call | solution.py:345
  36.3 1.3 %copy.4 = f32[1024]{0:T(1024)} copy(f32[1024]{0:T(1024)} %bitcast.2) | data formatting | bytes 8192
